TPU v7x, 32 devices: a whole 2x2x4 slice. The times are simulated.
32 devices in a mesh: dp: 4 (over x, core), expert: 8 (over z, y).
Axes of the slice: x: 2, y: 2, z: 4, core: 2. Of those that a mesh axis runs over, the one named last changes fastest.
Arguments:
- tokens: bfloat16 [4096, 4096], P(('dp', 'expert')), may hold values from -6 to 6
- router: bfloat16 [4096, 8], replicated, may hold values from -0.09375 to 0.09375
- price: float32 [8], replicated, may hold values from -1 to 1
- w_in: bfloat16 [8, 4096, 8192], P('expert', None, 'dp'), may hold values from -0.09375 to 0.09375
- w_out: bfloat16 [8, 8192, 4096], P('expert', 'dp'), may hold values from -0.0625 to 0.0625
- assign: int32 [4096], P(('dp', 'expert')), may hold values from 0 to 7, as said below
Outputs:
- mixed: bfloat16 [4096, 4096], P(('dp', 'expert'))
- new_price: float32 [8], replicated
Inputs may be any that keep to these rules, and one draw needn't show every extreme that they name: `assign`: every expert is named by exactly 512 tokens in all, and by at most 24 of the 128 tokens of one device (aligned blocks of 128 rows); on every device some expert is named exactly 24 times, and the experts' loads on one device are, in some order, the same 8 numbers on every device.
All inputs are finite; a program needn't handle non-finite values.
Results may differ from a plain program's by a relative error of at most 0.013.
Values may be sent and summed in bfloat16 or wider, within the bound.
A program may use at most 128 MiB of HBM per device.

v0:
```python
import jax
import jax.numpy as jnp
from jax import lax
from jax.sharding import PartitionSpec as P

BID_STEP = 0.01


def shards(tokens, router, price, w_in, w_out, assign):
    experts = router.shape[1]
    width = tokens.shape[1]
    local_tokens = tokens.shape[0]
    capacity = 3 * local_tokens // (2 * experts)
    dp_count = lax.axis_size("dp")
    first = w_in[0]
    second = w_out[0]
    affinity = jnp.dot(tokens, router, preferred_element_type=jnp.float32)
    onehot = assign[:, None] == jnp.arange(experts, dtype=jnp.int32)[None, :]
    own = jnp.sum(jnp.where(onehot, affinity, 0.0), axis=1)
    rival = jnp.max(jnp.where(onehot, -1e30, affinity - price[None, :]), axis=1)
    bid = own - rival + BID_STEP
    local_best = jnp.max(jnp.where(onehot, bid[:, None], -1e30), axis=0)
    new_price = lax.pmax(local_best, ("dp", "expert"))
    running = jnp.cumsum(onehot.astype(jnp.int32), axis=0)
    slots = jnp.sum(jnp.where(onehot, running, 0), axis=1) - 1
    buffer = jnp.zeros((experts, capacity, width), tokens.dtype).at[assign, slots].set(tokens)
    outgoing = jnp.broadcast_to(buffer[None], (dp_count,) + buffer.shape)
    outgoing = outgoing.reshape(dp_count * experts, capacity, width)
    raw = jnp.einsum(
        "scd,dh->sch",
        lax.all_to_all(outgoing, ("dp", "expert"), split_axis=0, concat_axis=0, tiled=True),
        first,
        preferred_element_type=jnp.float32,
    )
    hidden = jax.nn.gelu(raw, approximate=True).astype(jnp.bfloat16)
    flat_hidden = hidden.reshape(-1, hidden.shape[2])
    summed = lax.psum_scatter(
        jnp.dot(flat_hidden, second, preferred_element_type=jnp.float32).astype(jnp.bfloat16),
        "dp",
        scatter_dimension=0,
        tiled=True,
    )
    expert_out = summed.reshape(experts, capacity, width)
    returned = lax.all_to_all(expert_out, "expert", split_axis=0, concat_axis=0, tiled=True)
    picked = returned[assign, slots]
    gate = jax.nn.sigmoid(own)
    mixed = (gate[:, None] * picked.astype(jnp.float32)).astype(jnp.bfloat16)
    return (mixed, new_price)


def solution(mesh):
    return jax.shard_map(
        shards,
        mesh=mesh,
        in_specs=(
            P(("dp", "expert"), None),
            P(),
            P(),
            P("expert", None, "dp"),
            P("expert", "dp", None),
            P(("dp", "expert")),
        ),
        out_specs=(P(("dp", "expert"), None), P()),
        check_vma=False,
    )
```

profile of v0, /device:TPU:0, one launch (start us, length us, event | category | flops | bytes accessed | tf_op | source)
XLA Modules:
  0.0 349.4 jit_solution(10846029826754177063)
XLA Ops:
  7.2 0.0 copy-start
  7.2 0.0 reduce-scatter.2.cloned.1.call-start
  7.2 0.7 fusion.17
  7.9 0.1 copy.10
  8.0 0.2 reduce_window_sum.11
  8.2 0.7 select_reduce_fusion.2
  8.9 0.7 fusion.21
  9.6 0.2 broadcast_in_dim.43
  9.7 24.9 %scatter_fusion = bf16[8,24,4096]{2,1,0:T(8,128)(2,1)S(1)} fusion(bf16[8,24,4096]{2,1,0:T(8,128)(2,1)S(1)} %broadcast_in_dim.43, s32[128]{0:T(128)S(1)} %get-tuple-element.5, bf16[128,4096]{1,0:T(8,128)(2,1)} %param.6), kind=kCustom, calls=%fused_computation.1 | custom fusion | bytes 3146752 | tf_op jit(solution)/shard_map/scatter | solution.py:26
  34.6 0.8 broadcast_in_dim.46
  35.4 147.0 %all_to_all.10 = bf16[32,24,4096]{2,1,0:T(8,128)(2,1)S(1)} all-to-all(bf16[32,24,4096]{2,1,0:T(8,128)(2,1)S(1)} %bitcast.52), channel_id=1, replica_groups=mesh['dp'=4,'expert'=8] {'dp','expert'}, dimensions={0} | all-to-all | bytes 12582912 | tf_op jit(solution)/shard_map/all_to_all | solution.py:31
  182.5 17.9 %fusion.14 = bf16[32,24,2048]{2,1,0:T(8,128)(2,1)S(1)} fusion(bf16[32,24,4096]{2,1,0:T(8,128)(2,1)S(1)} %all_to_all.10, bf16[1,4096,2048]{2,1,0:T(8,128)(2,1)} %param.9), kind=kOutput, calls=%fused_computation.15 | convolution fusion | flops 12899057664 | bytes 26214400 | tf_op jit(solution)/shard_map/scd,dh->sch/dot_general | solution.py:29
  200.4 18.4 %fusion.4 = bf16[768,4096]{1,0:T(8,128)(2,1)} fusion(bf16[768,2048]{1,0:T(8,128)(2,1)S(1)} %bitcast.54, bf16[1,2048,4096]{2,1,0:T(8,128)(2,1)} %param.10), kind=kOutput, calls=%fused_computation.7 | convolution fusion | flops 12888047616 | bytes 26214400 | tf_op jit(solution)/shard_map/dot_general | solution.py:38
  218.8 0.0 copy-start.1
  218.8 0.0 copy-start.2
  218.8 0.0 copy-start.3
  218.8 0.0 reduce-scatter.2.cloned.1.call-update
  218.9 56.2 %reduce-scatter.2.cloned.1.call-done = bf16[192,4096]{1,0:T(8,128)(2,1)} async-done(((bf16[768,4096]{1,0:T(8,128)(2,1)}), bf16[192,4096]{1,0:T(8,128)(2,1)}) %reduce-scatter.2.cloned.1.call-update) | async-done | bytes 1572880 | tf_op jit(solution)/shard_map/reduce_scatter | solution.py:37
  275.0 5.5 %all-to-all-start.1 = ((bf16[8,24,4096]{2,1,0:T(8,128)(2,1)}), bf16[8,24,4096]{2,1,0:T(8,128)(2,1)S(1)}, u32[]{:S(2)}, u32[]{:S(2)}) async-start(bf16[8,24,4096]{2,1,0:T(8,128)(2,1)} %bitcast.53), calls=%async_computation.2 | async-start | bytes 3145728 | tf_op jit(solution)/shard_map/all_to_all | solution.py:44
  280.6 0.0 copy-done
  280.6 0.0 copy-done.1
  280.6 0.0 copy-done.2
  280.6 0.0 copy-done.3
  280.6 0.4 select_reduce_fusion.1
  281.0 0.1 select_reduce_fusion
  281.1 56.3 %pmax.7 = f32[8]{0:T(128)} all-reduce(f32[8]{0:T(128)S(1)} %select_reduce_fusion), channel_id=1, replica_groups=mesh['dp'=4,'expert'=8] {'dp','expert'}, use_global_device_ids=true, to_apply=%region_7.8 | all-reduce | flops 8 | bytes 64 | tf_op jit(solution)/shard_map/pmax | solution.py:23
  337.4 0.0 all-to-all-done.1
  337.4 3.9 %gather_fusion = bf16[128,4096]{1,0:T(8,128)(2,1)S(1)} fusion(bf16[8,24,4096]{2,1,0:T(8,128)(2,1)S(1)} %all-to-all-done.1, s32[128]{0:T(128)S(1)} %get-tuple-element.4), kind=kCustom, calls=%fused_computation | custom fusion | bytes 2098176 | tf_op jit(solution)/shard_map/gather | solution.py:45
  341.3 1.2 multiply_convert_fusion
  (2 shorter events, 0.1 us)
Async XLA Ops:
  7.2 273.4 %copy-start = (bf16[4096,8]{0,1:T(8,128)(2,1)S(1)}, bf16[4096,8]{0,1:T(8,128)(2,1)}, u32[]{:S(2)}) copy-start(bf16[4096,8]{0,1:T(8,128)(2,1)} %param.7) | copy-start | bytes 196612
  7.2 267.9 %reduce-scatter.2.cloned.1.call-start = ((), (), s32[]{:S(2)}) async-start(), calls=%async_computation.3 | async-start | bytes 7864320 | tf_op jit(solution)/shard_map/reduce_scatter | solution.py:37
  218.8 61.7 %copy-start.1 = (bf16[128,4096]{1,0:T(8,128)(2,1)S(1)}, bf16[128,4096]{1,0:T(8,128)(2,1)}, u32[]{:S(2)}) copy-start(bf16[128,4096]{1,0:T(8,128)(2,1)} %param.6) | copy-start | bytes 3145732
  218.8 61.8 %copy-start.2 = (s32[128]{0:T(128)S(1)}, s32[128]{0:T(128)}, u32[]{:S(2)}) copy-start(s32[128]{0:T(128)} %param.11) | copy-start | bytes 1540
  218.8 61.8 %copy-start.3 = (f32[8]{0:T(128)S(1)}, f32[8]{0:T(128)}, u32[]{:S(2)}) copy-start(f32[8]{0:T(128)} %param.8) | copy-start | bytes 100
  275.0 62.4 %all-to-all-start.1 = ((bf16[8,24,4096]{2,1,0:T(8,128)(2,1)}), bf16[8,24,4096]{2,1,0:T(8,128)(2,1)S(1)}, u32[]{:S(2)}, u32[]{:S(2)}) async-start(bf16[8,24,4096]{2,1,0:T(8,128)(2,1)} %bitcast.53), calls=%async_computation.2 | async-start | bytes 3145728 | tf_op jit(solution)/shard_map/all_to_all | solution.py:44
Sparse Core Ops, SparseCore 0:
  219.0 56.0 reduce-scatter.1
where the time goes:
time: 350 us; the launch traced here: 349 us
  blocking collectives  203 us (58%)
  waiting for transfers between devices  56.2 us (16%)
  matrix products  36.8 us (11%)
  local copies, waits for them, and re-layouts  29.9 us (9%)
  between operations  14.1 us (4%)
  starting transfers between devices  5.56 us (2%)
  other arithmetic  3.54 us (1%)
    all_to_all x1, blocking collectives, shards(): lax.all_to_all(outgoing, ('dp', 'expert'), split_axis=0, concat_axis=0, t...  147 us
    pmax x1, blocking collectives, shards(): new_price = lax.pmax(local_best, ('dp', 'expert'))  56.3 us
    reduce_scatter x1, waiting for transfers between devices, shards(): lax.psum_scatter(jnp.dot(flat_hidden, second, preferred_element_type=jnp....  56.2 us
    scatter x1, local copies, waits for them, and re-layouts, shards(): jnp.zeros((experts, capacity, width), tokens.dtype).at[assign, slots]  24.9 us
    dot_general x1, matrix products, shards(): jnp.dot(flat_hidden, second, preferred_element_type=jnp.float32)  18.4 us
    dot_general x1, matrix products, shards(): jnp.einsum('scd,dh->sch', lax.all_to_all(outgoing, ('dp', 'expert'), spli...  17.9 us
  transfers between devices with their start and end apart: 2, of which 1 were waited for; matrix products, arithmetic and copies ran while one was open for 0% of the time, Pallas kernels for 0%

commit v1 on v0

v1 whole, which is shorter than its diff:
```python
import jax
import jax.numpy as jnp
from jax import lax
from jax.sharding import PartitionSpec as P

BID_STEP = 0.01


def shards(tokens, router, price, w_in, w_out, assign):
    experts = router.shape[1]
    width = tokens.shape[1]
    local_tokens = tokens.shape[0]
    capacity = 3 * local_tokens // (2 * experts)
    first = w_in[0]
    second = w_out[0]
    affinity = jnp.dot(tokens, router, preferred_element_type=jnp.float32)
    onehot = assign[:, None] == jnp.arange(experts, dtype=jnp.int32)[None, :]
    own = jnp.sum(jnp.where(onehot, affinity, 0.0), axis=1)
    rival = jnp.max(jnp.where(onehot, -1e30, affinity - price[None, :]), axis=1)
    bid = own - rival + BID_STEP
    local_best = jnp.max(jnp.where(onehot, bid[:, None], -1e30), axis=0)
    new_price = lax.pmax(local_best, ("dp", "expert"))
    lower = (jnp.arange(local_tokens)[:, None] >= jnp.arange(local_tokens)[None, :]).astype(jnp.bfloat16)
    running = jnp.dot(lower, onehot.astype(jnp.bfloat16), preferred_element_type=jnp.float32)
    slots = jnp.sum(jnp.where(onehot, running, 0.0), axis=1).astype(jnp.int32) - 1
    place = assign * capacity + slots
    pack = (place[None, :] == jnp.arange(experts * capacity, dtype=jnp.int32)[:, None]).astype(jnp.bfloat16)
    packed = jnp.dot(pack, tokens, preferred_element_type=jnp.float32).astype(jnp.bfloat16)
    mine = lax.all_to_all(packed.reshape(experts, capacity, width), "expert", split_axis=0, concat_axis=0, tiled=True)
    rows = lax.all_gather(mine.reshape(experts * capacity, width), "dp", axis=0, tiled=True)
    raw = jnp.dot(rows, first, preferred_element_type=jnp.float32)
    hidden = jax.nn.gelu(raw, approximate=True).astype(jnp.bfloat16)
    partial = jnp.dot(hidden, second, preferred_element_type=jnp.float32).astype(jnp.bfloat16)
    summed = lax.psum_scatter(partial, "dp", scatter_dimension=0, tiled=True)
    returned = lax.all_to_all(
        summed.reshape(experts, capacity, width), "expert", split_axis=0, concat_axis=0, tiled=True
    ).reshape(experts * capacity, width)
    picked = lax.dot_general(pack, returned, (((0,), (0,)), ((), ())), preferred_element_type=jnp.float32)
    gate = jax.nn.sigmoid(own)
    mixed = (gate[:, None] * picked).astype(jnp.bfloat16)
    return (mixed, new_price)


def solution(mesh):
    return jax.shard_map(
        shards,
        mesh=mesh,
        in_specs=(
            P(("dp", "expert"), None),
            P(),
            P(),
            P("expert", None, "dp"),
            P("expert", "dp", None),
            P(("dp", "expert")),
        ),
        out_specs=(P(("dp", "expert"), None), P()),
        check_vma=False,
    )
```

time: 350 us -> 269 us (0.77)
  blocking collectives: 203 us -> 101 us
  waiting for transfers between devices: 56.2 us -> 104 us
  local copies, waits for them, and re-layouts: 29.9 us -> 0.03 us
  matrix products: 36.8 us -> 43.6 us
    all_to_all x1, blocking collectives: 147 us -> 44.2 us  [shards(): lax.all_to_all(packed.reshape(experts, capacity, width), 'expert', split_...]
    all_gather x0 -> x1, waiting for transfers between devices: none -> 45.5 us  [shards(): lax.all_gather(mine.reshape(experts * capacity, width), 'dp', axis=0, til...]
    scatter x1 -> x0, local copies, waits for them, and re-layouts: 24.9 us -> none  [shards(): jnp.zeros((experts, capacity, width), tokens.dtype).at[assign, slots]]
    dot_general x2 -> x4, matrix products: 36.4 us -> 43.2 us  [the longest x1 40.2 us: shards(): jnp.dot(hidden, second, preferred_element_type=jnp.float32)]
    gather x1 -> x0, local copies, waits for them, and re-layouts: 3.88 us -> none  [shards(): picked = returned[assign, slots]]
  transfers between devices with their start and end apart: 2 -> 3, of which waited for: 1 -> 2; matrix products, arithmetic and copies ran while one was open for 0% -> 0% of each run, Pallas kernels for 0% -> 0%
where the time goes in v1:
time: 269 us
  waiting for transfers between devices  104 us (39%)
  blocking collectives  101 us (38%)
  matrix products  43.6 us (16%)
  between operations  14.1 us (5%)
  starting transfers between devices  5.59 us (2%)
    reduce_scatter x1, waiting for transfers between devices, shards(): summed = lax.psum_scatter(partial, 'dp', scatter_dimension=0, tiled=True)  58.5 us
    pmax x1, blocking collectives, shards(): new_price = lax.pmax(local_best, ('dp', 'expert'))  56.3 us
    all_gather x1, waiting for transfers between devices, shards(): lax.all_gather(mine.reshape(experts * capacity, width), 'dp', axis=0, til...  45.5 us
    all_to_all x1, blocking collectives, shards(): lax.all_to_all(packed.reshape(experts, capacity, width), 'expert', split_...  44.2 us
    dot_general x1, matrix products, shards(): jnp.dot(hidden, second, preferred_element_type=jnp.float32)  40.2 us
    all_to_all x1, starting transfers between devices, shards(): lax.all_to_all(summed.reshape(experts, capacity, width), 'expert', split_...  5.51 us
  transfers between devices with their start and end apart: 3, of which 2 were waited for; matrix products, arithmetic and copies ran while one was open for 0% of the time, Pallas kernels for 0%

profile of v1, /device:TPU:0, one launch (start us, length us, event | category | flops | bytes accessed | tf_op | source)
XLA Modules:
  0.0 268.7 jit_solution(14354729918108742788)
XLA Ops:
  7.2 0.0 copy-start
  7.2 0.0 all-gather.2.cloned.1.call-start
  7.2 0.9 fusion.21
  8.1 0.7 add_add_fusion
  8.8 0.0 copy-done
  8.8 0.0 copy-start.2
  8.8 0.6 convolution_convert_fusion
  9.4 44.2 %all_to_all.10 = bf16[8,24,4096]{2,1,0:T(8,128)(2,1)} all-to-all(bf16[8,24,4096]{2,1,0:T(8,128)(2,1)S(1)} %bitcast.23), channel_id=1, replica_groups=mesh['dp'=4,'expert'=8] {'expert'}, dimensions={0} | all-to-all | bytes 3145728 | tf_op jit(solution)/shard_map/all_to_all | solution.py:29
  53.6 0.0 copy-done.2
  53.6 0.0 all-gather.2.cloned.1.call-update
  53.6 0.0 reduce-scatter.2.cloned.1.call-start
  53.6 45.5 %all-gather.2.cloned.1.call-done = bf16[768,4096]{1,0:T(8,128)(2,1)} async-done(((bf16[192,4096]{1,0:T(8,128)(2,1)}), bf16[768,4096]{1,0:T(8,128)(2,1)}) %all-gather.2.cloned.1.call-update) | async-done | bytes 6291472 | tf_op jit(solution)/shard_map/all_gather | solution.py:30
  99.1 40.2 %fusion.4 = bf16[768,4096]{1,0:T(8,128)(2,1)} fusion(bf16[1,2048,4096]{2,1,0:T(8,128)(2,1)} %param.10, bf16[768,4096]{1,0:T(8,128)(2,1)} %all-gather.2.cloned.1.call-done, bf16[1,4096,2048]{2,1,0:T(8,128)(2,1)} %param.9), kind=kOutput, calls=%fused_computation.5 | convolution fusion | flops 25787105280 | bytes 46137344 | tf_op jit(solution)/shard_map/dot_general | solution.py:33
  139.4 0.0 copy-start.1
  139.4 0.0 copy-start.4
  139.4 0.0 copy-start.5
  139.4 0.0 copy-start.3
  139.4 0.0 reduce-scatter.2.cloned.1.call-update
  139.4 58.5 %reduce-scatter.2.cloned.1.call-done = bf16[192,4096]{1,0:T(8,128)(2,1)} async-done(((bf16[768,4096]{1,0:T(8,128)(2,1)}), bf16[192,4096]{1,0:T(8,128)(2,1)}) %reduce-scatter.2.cloned.1.call-update) | async-done | bytes 1572880 | tf_op jit(solution)/shard_map/reduce_scatter | solution.py:34
  197.9 5.5 %all-to-all-start.1 = ((bf16[8,24,4096]{2,1,0:T(8,128)(2,1)}), bf16[8,24,4096]{2,1,0:T(8,128)(2,1)S(1)}, u32[]{:S(2)}, u32[]{:S(2)}) async-start(bf16[8,24,4096]{2,1,0:T(8,128)(2,1)} %bitcast.24), calls=%async_computation.2 | async-start | bytes 3145728 | tf_op jit(solution)/shard_map/all_to_all | solution.py:35
  203.5 0.0 copy-done.1
  203.5 0.0 copy-done.4
  203.5 0.0 copy-done.5
  203.5 0.4 select_reduce_fusion.1
  203.9 0.1 select_reduce_fusion
  204.0 56.3 %pmax.7 = f32[8]{0:T(128)} all-reduce(f32[8]{0:T(128)S(1)} %select_reduce_fusion), channel_id=1, replica_groups=mesh['dp'=4,'expert'=8] {'dp','expert'}, use_global_device_ids=true, to_apply=%region_5.6 | all-reduce | flops 8 | bytes 64 | tf_op jit(solution)/shard_map/pmax | solution.py:22
  260.3 0.0 all-to-all-done.1
  260.3 0.0 copy-done.3
  260.3 1.5 fusion.15
  (1 shorter events, 0.0 us)
Async XLA Ops:
  7.2 1.6 copy-start
  7.2 92.0 %all-gather.2.cloned.1.call-start = ((), (), s32[]{:S(2)}) async-start(), calls=%async_computation.3 | async-start | bytes 7864320 | tf_op jit(solution)/shard_map/all_gather | solution.py:30
  8.8 44.8 %copy-start.2 = (s32[128]{0:T(128)}, s32[128]{0:T(128)S(1)}, u32[]{:S(2)}) copy-start(s32[128]{0:T(128)S(1)} %add_add_fusion) | copy-start | bytes 1540
  53.6 144.3 %reduce-scatter.2.cloned.1.call-start = ((), (), s32[]{:S(2)}) async-start(), calls=%async_computation.4 | async-start | bytes 7864320 | tf_op jit(solution)/shard_map/reduce_scatter | solution.py:34
  139.4 64.1 %copy-start.1 = (bf16[4096,8]{0,1:T(8,128)(2,1)S(1)}, bf16[4096,8]{0,1:T(8,128)(2,1)}, u32[]{:S(2)}) copy-start(bf16[4096,8]{0,1:T(8,128)(2,1)} %param.7) | copy-start | bytes 196612
  139.4 64.1 %copy-start.4 = (f32[8]{0:T(128)S(1)}, f32[8]{0:T(128)}, u32[]{:S(2)}) copy-start(f32[8]{0:T(128)} %param.8) | copy-start | bytes 100
  139.4 64.1 %copy-start.5 = (s32[128]{0:T(128)S(1)}, s32[128]{0:T(128)}, u32[]{:S(2)}) copy-start(s32[128]{0:T(128)} %param.11) | copy-start | bytes 1540
  139.4 121.0 %copy-start.3 = (s32[128]{0:T(128)S(1)}, s32[128]{0:T(128)}, u32[]{:S(2)}) copy-start(s32[128]{0:T(128)} %copy-done.2) | copy-start | bytes 1540
  197.9 62.4 %all-to-all-start.1 = ((bf16[8,24,4096]{2,1,0:T(8,128)(2,1)}), bf16[8,24,4096]{2,1,0:T(8,128)(2,1)S(1)}, u32[]{:S(2)}, u32[]{:S(2)}) async-start(bf16[8,24,4096]{2,1,0:T(8,128)(2,1)} %bitcast.24), calls=%async_computation.2 | async-start | bytes 3145728 | tf_op jit(solution)/shard_map/all_to_all | solution.py:35
Sparse Core Ops, SparseCore 0:
  53.7 45.3 all-gather.1
  139.5 58.3 reduce-scatter.1

commit v2 on v1

v2 whole, which is shorter than its diff:
```python
import functools

import jax
import jax.numpy as jnp
from jax import lax
from jax.experimental import pallas as pl
from jax.experimental.pallas import tpu as pltpu
from jax.sharding import PartitionSpec as P

BID_STEP = 0.01
MESH = pl.DeviceIdType.MESH


def remote(src, dst, send, recv, a, b):
    return pltpu.make_async_remote_copy(
        src_ref=src, dst_ref=dst, send_sem=send, recv_sem=recv, device_id=(a, b), device_id_type=MESH
    )


def greet(dps, experts, a, b):
    barrier = pltpu.get_barrier_semaphore()
    for k in range(1, experts):
        pl.semaphore_signal(barrier, inc=1, device_id=(a, lax.rem(b + k, experts)), device_id_type=MESH)
    for k in range(1, dps):
        pl.semaphore_signal(barrier, inc=1, device_id=(lax.rem(a + k, dps), b), device_id_type=MESH)
    pl.semaphore_wait(barrier, experts + dps - 2)


def dispatch_kernel(dps, experts, packed, best, rows, bests, own_sem, s1, r1, s2, r2, s3, r3, sb, rb):
    a, b = lax.axis_index("dp"), lax.axis_index("expert")
    nx = dps // 2
    x, c = a // 2, lax.rem(a, 2)
    other = 2 * x + 1 - c
    greet(dps, experts, a, b)
    own = pltpu.make_async_copy(packed.at[b], rows.at[a, b], own_sem.at[0])
    own_best = pltpu.make_async_copy(best, bests.at[b], own_sem.at[1])
    own.start()
    own_best.start()

    def out(k):
        e = lax.rem(b + k, experts)
        return remote(packed.at[e], rows.at[a, b], s1.at[k], r1.at[k], a, e)

    def out_best(k):
        e = lax.rem(b + k, experts)
        return remote(best, bests.at[b], sb.at[k], rb.at[k], a, e)

    def source(k):
        return lax.rem(b + experts - k, experts)

    def across(q, k):
        to = 2 * lax.rem(x + q, nx) + c
        s = source(k)
        return remote(rows.at[a, s], rows.at[a, s], s2.at[q - 1, k], r2.at[q - 1, k], to, b)

    def beside(q, k):
        row = 2 * lax.rem(x + nx - q, nx) + c
        s = source(k)
        return remote(rows.at[row, s], rows.at[row, s], s3.at[q, k], r3.at[q, k], other, b)

    for k in range(1, experts):
        out(k).start()
    for k in range(1, experts):
        out_best(k).start()
    for k in range(experts):
        s = source(k)
        if k == 0:
            own.wait()
        else:
            remote(packed.at[s], rows.at[a, s], s1.at[k], r1.at[k], a, s).wait_recv()
        for q in range(1, nx):
            across(q, k).start()
        beside(0, k).start()
    for k in range(experts):
        s = source(k)
        for q in range(1, nx):
            row = 2 * lax.rem(x + nx - q, nx) + c
            remote(rows.at[row, s], rows.at[row, s], s2.at[q - 1, k], r2.at[q - 1, k], row, b).wait_recv()
            beside(q, k).start()
    for k in range(experts):
        s = source(k)
        for q in range(nx):
            row = 2 * lax.rem(x + nx - q, nx) + 1 - c
            remote(rows.at[row, s], rows.at[row, s], s3.at[q, k], r3.at[q, k], other, b).wait_recv()
    own_best.wait()
    for k in range(1, experts):
        s = source(k)
        remote(best, bests.at[s], sb.at[k], rb.at[k], a, s).wait_recv()
        out_best(k).wait_send()
        out(k).wait_send()
    for k in range(experts):
        for q in range(1, nx):
            across(q, k).wait_send()
        for q in range(nx):
            beside(q, k).wait_send()


def dispatch(packed, best, dps):
    experts, capacity, width = packed.shape
    nx = dps // 2
    sem = pltpu.SemaphoreType.DMA
    return pl.pallas_call(
        functools.partial(dispatch_kernel, dps, experts),
        out_shape=(
            jax.ShapeDtypeStruct((dps, experts, capacity, width), packed.dtype),
            jax.ShapeDtypeStruct((experts,) + best.shape, best.dtype),
        ),
        in_specs=[pl.BlockSpec(memory_space=pl.ANY)] * 2,
        out_specs=(pl.BlockSpec(memory_space=pl.ANY),) * 2,
        scratch_shapes=[
            sem((2,)),
            sem((experts,)),
            sem((experts,)),
            sem((nx - 1, experts)),
            sem((nx - 1, experts)),
            sem((nx, experts)),
            sem((nx, experts)),
            sem((experts,)),
            sem((experts,)),
        ],
        compiler_params=pltpu.CompilerParams(collective_id=0, has_side_effects=True),
        name="dispatch",
    )(packed, best)


def collect_kernel(
    dps, experts, part, best, back, bests, pair, far, final, own_sem, s1, r1, s2, r2, s3, r3, sb, rb
):
    a, b = lax.axis_index("dp"), lax.axis_index("expert")
    nx = dps // 2
    x, c = a // 2, lax.rem(a, 2)
    other = 2 * x + 1 - c
    width = part.shape[3]
    piece = width // 4
    greet(dps, experts, a, b)
    own_best = pltpu.make_async_copy(best, bests.at[a], own_sem.at[1])
    own_best.start()
    own = pltpu.make_async_copy(final.at[b], back.at[b], own_sem.at[0])

    def dest(k):
        return lax.rem(b + k, experts)

    def beside(q, k):
        s = dest(k)
        return remote(
            part.at[2 * lax.rem(x + q, nx) + 1 - c, s], pair.at[q, s], s1.at[q, k], r1.at[q, k], other, b
        )

    def across(q, k):
        s = dest(k)
        to = 2 * lax.rem(x + q, nx) + c
        return remote(pair.at[q, s], far.at[q - 1, s], s2.at[q - 1, k], r2.at[q - 1, k], to, b)

    def home(k):
        s = dest(k)
        return remote(final.at[s], back.at[b], s3.at[k], r3.at[k], a, s)

    def out_best(k):
        return remote(best, bests.at[a], sb.at[k], rb.at[k], lax.rem(a + k, dps), b)

    order = list(range(1, experts)) + [0]
    for k in order:
        for q in range(1, nx):
            beside(q, k).start()
    for k in order:
        beside(0, k).start()
    for k in range(1, dps):
        out_best(k).start()
    for k in order:
        s = dest(k)
        for q in range(1, nx):
            row = 2 * lax.rem(x + q, nx) + c
            beside(q, k).wait_recv()
            for p in range(4):
                cols = pl.ds(p * piece, piece)
                total = part[row, s, :, cols].astype(jnp.float32) + pair[q, s, :, cols].astype(jnp.float32)
                pair[q, s, :, cols] = total.astype(jnp.bfloat16)
            across(q, k).start()
    for k in order:
        s = dest(k)
        beside(0, k).wait_recv()
        for q in range(1, nx):
            across(q, k).wait_recv()
        for p in range(4):
            cols = pl.ds(p * piece, piece)
            total = part[a, s, :, cols].astype(jnp.float32) + pair[0, s, :, cols].astype(jnp.float32)
            for q in range(1, nx):
                total = total + far[q - 1, s, :, cols].astype(jnp.float32)
            final[s, :, cols] = total.astype(jnp.bfloat16)
        if k == 0:
            own.start()
        else:
            home(k).start()
    own.wait()
    own_best.wait()
    for k in range(1, dps):
        s = lax.rem(a + dps - k, dps)
        remote(best, bests.at[s], sb.at[k], rb.at[k], s, b).wait_recv()
        out_best(k).wait_send()
    for k in range(1, experts):
        s = lax.rem(b + experts - k, experts)
        remote(final.at[s], back.at[s], s3.at[k], r3.at[k], a, s).wait_recv()
        home(k).wait_send()
    for k in range(experts):
        for q in range(nx):
            beside(q, k).wait_send()
        for q in range(1, nx):
            across(q, k).wait_send()


def collect(part, best):
    dps, experts, capacity, width = part.shape
    nx = dps // 2
    sem = pltpu.SemaphoreType.DMA
    return pl.pallas_call(
        functools.partial(collect_kernel, dps, experts),
        out_shape=(
            jax.ShapeDtypeStruct((experts, capacity, width), part.dtype),
            jax.ShapeDtypeStruct((dps,) + best.shape, best.dtype),
        ),
        in_specs=[pl.BlockSpec(memory_space=pltpu.VMEM), pl.BlockSpec(memory_space=pl.ANY)],
        out_specs=(pl.BlockSpec(memory_space=pl.ANY),) * 2,
        scratch_shapes=[
            pltpu.VMEM((nx, experts, capacity, width), part.dtype),
            pltpu.VMEM((nx - 1, experts, capacity, width), part.dtype),
            pltpu.VMEM((experts, capacity, width), part.dtype),
            sem((2,)),
            sem((nx, experts)),
            sem((nx, experts)),
            sem((nx - 1, experts)),
            sem((nx - 1, experts)),
            sem((experts,)),
            sem((experts,)),
            sem((dps,)),
            sem((dps,)),
        ],
        compiler_params=pltpu.CompilerParams(
            collective_id=1, has_side_effects=True, vmem_limit_bytes=60 * 1024 * 1024
        ),
        name="collect",
    )(part, best)


def shards(tokens, router, price, w_in, w_out, assign):
    experts = router.shape[1]
    width = tokens.shape[1]
    local_tokens = tokens.shape[0]
    capacity = 3 * local_tokens // (2 * experts)
    dp_count = lax.axis_size("dp")
    first = w_in[0]
    second = w_out[0]
    affinity = jnp.dot(tokens, router, preferred_element_type=jnp.float32)
    onehot = assign[:, None] == jnp.arange(experts, dtype=jnp.int32)[None, :]
    own = jnp.sum(jnp.where(onehot, affinity, 0.0), axis=1)
    rival = jnp.max(jnp.where(onehot, -1e30, affinity - price[None, :]), axis=1)
    bid = own - rival + BID_STEP
    local_best = jnp.max(jnp.where(onehot, bid[:, None], -1e30), axis=0)
    lower = (jnp.arange(local_tokens)[:, None] >= jnp.arange(local_tokens)[None, :]).astype(jnp.bfloat16)
    running = jnp.dot(lower, onehot.astype(jnp.bfloat16), preferred_element_type=jnp.float32)
    slots = jnp.sum(jnp.where(onehot, running, 0.0), axis=1).astype(jnp.int32) - 1
    place = assign * capacity + slots
    pack = (place[None, :] == jnp.arange(experts * capacity, dtype=jnp.int32)[:, None]).astype(jnp.bfloat16)
    packed = jnp.dot(pack, tokens, preferred_element_type=jnp.float32).astype(jnp.bfloat16)
    best = jnp.full((8, 128), -1e30, jnp.float32).at[0, :experts].set(local_best)
    rows, bests = dispatch(packed.reshape(experts, capacity, width), best, dp_count)
    rows = rows.reshape(dp_count * experts * capacity, width)
    raw = jnp.dot(rows, first, preferred_element_type=jnp.float32)
    hidden = jax.nn.gelu(raw, approximate=True).astype(jnp.bfloat16)
    partial = jnp.dot(hidden, second, preferred_element_type=jnp.float32).astype(jnp.bfloat16)
    returned, all_bests = collect(
        partial.reshape(dp_count, experts, capacity, width), jnp.max(bests, axis=0)
    )
    new_price = jnp.max(all_bests, axis=0)[0, :experts]
    returned = returned.reshape(experts * capacity, width)
    picked = lax.dot_general(pack, returned, (((0,), (0,)), ((), ())), preferred_element_type=jnp.float32)
    gate = jax.nn.sigmoid(own)
    mixed = (gate[:, None] * picked).astype(jnp.bfloat16)
    return (mixed, new_price)


def solution(mesh):
    return jax.shard_map(
        shards,
        mesh=mesh,
        in_specs=(
            P(("dp", "expert"), None),
            P(),
            P(),
            P("expert", None, "dp"),
            P("expert", "dp", None),
            P(("dp", "expert")),
        ),
        out_specs=(P(("dp", "expert"), None), P()),
        check_vma=False,
    )
```

time: 269 us -> 166 us (0.62)
  Pallas kernels: 0 us -> 111 us
  waiting for transfers between devices: 104 us -> 0 us
  blocking collectives: 101 us -> 0 us
  between operations: 14.1 us -> 0.7 us
  starting transfers between devices: 5.59 us -> 0 us
  matrix products: 43.6 us -> 47 us
    pallas_call x0 -> x2, Pallas kernels: none -> 111 us  [the longest x1 57.4 us: collect(): pl.pallas_call(functools.partial(collect_kernel, dps, experts), out_shape...]
    reduce_scatter x1 -> x0, waiting for transfers between devices: 58.5 us -> none  [shards(): summed = lax.psum_scatter(partial, 'dp', scatter_dimension=0, tiled=True)]
    pmax x1 -> x0, blocking collectives: 56.3 us -> none  [shards(): new_price = lax.pmax(local_best, ('dp', 'expert'))]
    all_gather x1 -> x0, waiting for transfers between devices: 45.5 us -> none  [shards(): lax.all_gather(mine.reshape(experts * capacity, width), 'dp', axis=0, til...]
    all_to_all x1 -> x0, blocking collectives: 44.2 us -> none  [shards(): lax.all_to_all(packed.reshape(experts, capacity, width), 'expert', split_...]
    all_to_all x1 -> x0, starting transfers between devices: 5.51 us -> none  [shards(): lax.all_to_all(summed.reshape(experts, capacity, width), 'expert', split_...]
  transfers between devices with their start and end apart: 3 -> 0, of which waited for: 2 -> 0; matrix products, arithmetic and copies ran while one was open for 0% -> 0% of each run, Pallas kernels for 0% -> 0%
where the time goes in v2:
time: 166 us; the launch traced here: 163 us
  Pallas kernels  111 us (67%)
  matrix products  47 us (28%)
  other arithmetic  3.31 us (2%)
    pallas_call x1, Pallas kernels, collect(): pl.pallas_call(functools.partial(collect_kernel, dps, experts), out_shape...  57.4 us
    pallas_call x1, Pallas kernels, dispatch(): pl.pallas_call(functools.partial(dispatch_kernel, dps, experts), out_shap...  53.8 us
    dot_general x1, matrix products, shards(): jnp.dot(hidden, second, preferred_element_type=jnp.float32)  40.3 us

profile of v2, /device:TPU:0, one launch (start us, length us, event | category | flops | bytes accessed | tf_op | source)
XLA Modules:
  0.0 163.4 jit_solution(3234796675563684947)
XLA Ops:
  0.6 0.0 copy-start
  0.6 0.9 fusion.21
  1.6 0.7 add_add_fusion
  2.2 0.0 copy-done
  2.2 0.0 copy-start.3
  2.2 1.2 select_reduce_fusion.1
  3.5 0.5 add_divide_fusion
  4.0 0.8 select_reduce_fusion
  4.8 0.6 scatter.4.best
  5.4 0.0 copy-done.3
  5.4 1.7 %convolution_convert_fusion = bf16[192,4096]{1,0:T(8,128)(2,1)} fusion(bf16[128,4096]{1,0:T(8,128)(2,1)S(1)} %copy-done, s32[128]{0:T(128)S(1)} %add_add_fusion), kind=kOutput, calls=%fused_computation.14 | convolution fusion | flops 202137600 | bytes 2621952 | tf_op jit(solution)/shard_map/dot_general | solution.py:263
  7.1 53.8 %dispatch.1 = (bf16[4,8,24,4096]{3,2,1,0:T(8,128)(2,1)}, f32[8,8,128]{2,1,0:T(8,128)}) custom-call(bf16[8,24,4096]{2,1,0:T(8,128)(2,1)} %bitcast.24, f32[8,128]{1,0:T(8,128)} %scatter.4.best), custom_call_target="tpu_custom_call" | custom-call | tf_op jit(solution)/shard_map/dispatch/pallas_call | solution.py:102
  60.9 0.0 copy-start.1
  60.9 40.3 %fusion.4 = bf16[768,4096]{1,0:T(8,128)(2,1)} fusion(bf16[1,2048,4096]{2,1,0:T(8,128)(2,1)} %param.12, bf16[768,4096]{1,0:T(8,128)(2,1)} %bitcast.28, bf16[1,4096,2048]{2,1,0:T(8,128)(2,1)} %param.11), kind=kOutput, calls=%fused_computation.5 | convolution fusion | flops 25787105280 | bytes 46137344 | tf_op jit(solution)/shard_map/dot_general | solution.py:269
  101.2 0.0 copy-start.2
  101.2 0.0 copy-start.4
  101.2 0.0 copy-done.1
  101.2 0.6 reduce_max.38.best
  101.8 57.4 %collect.1 = (bf16[8,24,4096]{2,1,0:T(8,128)(2,1)}, f32[4,8,128]{2,1,0:T(8,128)}) custom-call(bf16[4,8,24,4096]{3,2,1,0:T(8,128)(2,1)} %bitcast.25, f32[8,128]{1,0:T(8,128)} %reduce_max.38.best), custom_call_target="tpu_custom_call" | custom-call | tf_op jit(solution)/shard_map/collect/pallas_call | solution.py:215
  159.3 0.0 copy-done.2
  159.3 0.0 copy-done.4
  159.3 2.9 %fusion.15 = bf16[128,4096]{1,0:T(8,128)(2,1)} fusion(bf16[192,4096]{1,0:T(8,128)(2,1)} %bitcast.26, f32[128]{0:T(128)S(1)} %copy-done.2, s32[128]{0:T(128)S(1)} %copy-done.4), kind=kOutput, calls=%fused_computation.16 | convolution fusion | flops 202399744 | bytes 2622464 | tf_op jit(solution)/shard_map/dot_general | solution.py:275
  162.1 0.7 reduce_max.39
  162.9 0.5 slice_bitcast_fusion
Async XLA Ops:
  0.6 1.6 copy-start
  2.2 3.2 %copy-start.3 = (s32[128]{0:T(128)}, s32[128]{0:T(128)S(1)}, u32[]{:S(2)}) copy-start(s32[128]{0:T(128)S(1)} %add_add_fusion) | copy-start | bytes 1540
  60.9 40.3 %copy-start.1 = (f32[8,8,128]{2,1,0:T(8,128)S(1)}, f32[8,8,128]{2,1,0:T(8,128)}, u32[]{:S(2)}) copy-start(f32[8,8,128]{2,1,0:T(8,128)} %get-tuple-element.19) | copy-start | bytes 98308
  101.2 58.1 %copy-start.2 = (f32[128]{0:T(128)S(1)}, f32[128]{0:T(128)}, u32[]{:S(2)}) copy-start(f32[128]{0:T(128)} %get-tuple-element.24) | copy-start | bytes 1540
  101.2 58.1 %copy-start.4 = (s32[128]{0:T(128)S(1)}, s32[128]{0:T(128)}, u32[]{:S(2)}) copy-start(s32[128]{0:T(128)} %copy-done.3) | copy-start | bytes 1540

commit v3 on v1

v3 whole, which is shorter than its diff:
```python
import functools

import jax
import jax.numpy as jnp
from jax import lax
from jax.experimental import pallas as pl
from jax.experimental.pallas import tpu as pltpu
from jax.sharding import PartitionSpec as P

BID_STEP = 0.01
MESH = pl.DeviceIdType.MESH


def remote(src, dst, send, recv, a, b):
    return pltpu.make_async_remote_copy(
        src_ref=src, dst_ref=dst, send_sem=send, recv_sem=recv, device_id=(a, b), device_id_type=MESH
    )


def greet(dps, experts, a, b):
    barrier = pltpu.get_barrier_semaphore()
    for k in range(1, experts):
        pl.semaphore_signal(barrier, inc=1, device_id=(a, lax.rem(b + k, experts)), device_id_type=MESH)
    for k in range(1, dps):
        pl.semaphore_signal(barrier, inc=1, device_id=(lax.rem(a + k, dps), b), device_id_type=MESH)
    pl.semaphore_wait(barrier, experts + dps - 2)


def layer_kernel(
    dps, experts, packed, best, w_in, w_out, back, rows, bests, all_bests,
    win, wout, loaded, flat, hidden, part, pair, far, final, top,
    load_sem, own_sem, s1, r1, s2, r2, s3, r3, s4, r4, s5, r5, s6, r6, sb, rb, sd, rd,
):
    a, b = lax.axis_index("dp"), lax.axis_index("expert")
    nx, groups = dps // 2, experts // 2
    x, c = a // 2, lax.rem(a, 2)
    z, y = b // 2, lax.rem(b, 2)
    other = 2 * x + 1 - c
    capacity, width = packed.shape[1:]
    ff = win.shape[1]
    cut = 512
    tall = 2 * dps * capacity
    load_in = pltpu.make_async_copy(w_in, win, load_sem.at[0])
    load_out = pltpu.make_async_copy(w_out, wout, load_sem.at[1])
    load_in.start()
    greet(dps, experts, a, b)

    def ahead(k):
        return 2 * lax.rem(z + k // 2, groups) + lax.rem(y + k % 2, 2)

    def behind(k):
        return 2 * lax.rem(z + groups - k // 2, groups) + lax.rem(y + k % 2, 2)

    def xrow(q):
        return 2 * lax.rem(x + q, nx) + c

    def xback(q):
        return 2 * lax.rem(x + nx - q, nx) + c

    def out(k):
        e = ahead(k)
        return remote(packed.at[e], rows.at[k, a], s1.at[k], r1.at[k], a, e)

    def out_best(k):
        return remote(best, bests.at[k], sb.at[k], rb.at[k], a, ahead(k))

    def spread_best(k):
        return remote(top, all_bests.at[k], sd.at[k], rd.at[k], lax.rem(a + k, dps), b)

    def fan(q, k):
        return remote(rows.at[k, a], rows.at[k, a], s2.at[q - 1, k], r2.at[q - 1, k], xrow(q), b)

    def fan_in(q, k):
        row = xback(q)
        return remote(rows.at[k, row], rows.at[k, row], s2.at[q - 1, k], r2.at[q - 1, k], row, b)

    def share(q, k):
        row = xback(q)
        return remote(rows.at[k, row], rows.at[k, row], s3.at[q, k], r3.at[q, k], other, b)

    def share_in(q, k):
        row = xback(q) + 1 - 2 * c
        return remote(rows.at[k, row], rows.at[k, row], s3.at[q, k], r3.at[q, k], other, b)

    def beside(q, k):
        return remote(
            part.at[k, xrow(q) + 1 - 2 * c], pair.at[q, k], s4.at[q, k], r4.at[q, k], other, b
        )

    def across(q, k):
        return remote(pair.at[q, k], far.at[q - 1, k], s5.at[q - 1, k], r5.at[q - 1, k], xrow(q), b)

    def home(k):
        return remote(final.at[k], back.at[b], s6.at[k], r6.at[k], a, behind(k))

    own = pltpu.make_async_copy(packed.at[b], rows.at[0, a], own_sem.at[0])
    own_back = pltpu.make_async_copy(final.at[0], back.at[b], own_sem.at[2])

    def arrive(g):
        for k in (2 * g, 2 * g + 1):
            if k == 0:
                own.wait()
            else:
                out(k).wait_recv()
            for q in range(1, nx):
                fan(q, k).start()
            share(0, k).start()

    def forward(g):
        for k in (2 * g, 2 * g + 1):
            for q in range(1, nx):
                fan_in(q, k).wait_recv()
                share(q, k).start()

    def compute(g):
        for k in (2 * g, 2 * g + 1):
            for q in range(nx):
                share_in(q, k).wait_recv()
        load = pltpu.make_async_copy(rows.at[pl.ds(2 * g, 2)], loaded, own_sem.at[1])
        load.start()
        load.wait()

        def flatten(t, carry):
            cols = pl.ds(pl.multiple_of(t * cut, cut), cut)
            block = loaded[:, :, :, cols].astype(jnp.float32)
            flat[:, cols] = block.reshape(tall, cut).astype(jnp.bfloat16)
            return carry

        def first(t, carry):
            cols = pl.ds(pl.multiple_of(t * cut, cut), cut)
            raw = jnp.dot(flat[...], win[:, cols], preferred_element_type=jnp.float32)
            hidden[:, cols] = jax.nn.gelu(raw, approximate=True).astype(jnp.bfloat16)
            return carry

        def second(t, carry):
            cols = pl.ds(pl.multiple_of(t * cut, cut), cut)
            res = jnp.dot(hidden[...], wout[:, cols], preferred_element_type=jnp.float32)
            part[2 * g : 2 * g + 2, :, :, cols] = res.reshape(2, dps, capacity, cut).astype(jnp.bfloat16)
            return carry

        lax.fori_loop(0, width // cut, flatten, 0)
        if g == 0:
            load_in.wait()
        lax.fori_loop(0, ff // cut, first, 0)
        if g == 0:
            load_out.wait()
        lax.fori_loop(0, width // cut, second, 0)
        for q in list(range(1, nx)) + [0]:
            for k in (2 * g, 2 * g + 1):
                beside(q, k).start()

    def add_pair(g):
        for k in (2 * g, 2 * g + 1):
            for q in range(1, nx):
                beside(q, k).wait_recv()

                def add(t, carry):
                    cols = pl.ds(pl.multiple_of(t * cut, cut), cut)
                    total = part[k, xrow(q), :, cols].astype(jnp.float32)
                    total = total + pair[q, k, :, cols].astype(jnp.float32)
                    pair[q, k, :, cols] = total.astype(jnp.bfloat16)
                    return carry

                lax.fori_loop(0, width // cut, add, 0)
                across(q, k).start()

    def add_far(g):
        for k in (2 * g, 2 * g + 1):
            beside(0, k).wait_recv()
            for q in range(1, nx):
                across(q, k).wait_recv()

            def add(t, carry):
                cols = pl.ds(pl.multiple_of(t * cut, cut), cut)
                total = part[k, a, :, cols].astype(jnp.float32)
                total = total + pair[0, k, :, cols].astype(jnp.float32)
                for q in range(1, nx):
                    total = total + far[q - 1, k, :, cols].astype(jnp.float32)
                final[k, :, cols] = total.astype(jnp.bfloat16)
                return carry

            lax.fori_loop(0, width // cut, add, 0)
            if k == 0:
                own_back.start()
            else:
                home(k).start()

    own.start()
    for k in range(1, experts):
        out(k).start()
    for k in range(1, experts):
        out_best(k).start()
    load_out.start()
    arrive(0)
    arrive(1)
    forward(0)
    for g in range(groups):
        compute(g)
        if g + 2 < groups:
            arrive(g + 2)
        if g + 1 < groups:
            forward(g + 1)
        if g >= 1:
            add_pair(g - 1)
        if g >= 2:
            add_far(g - 2)
    add_pair(groups - 1)
    for k in range(1, experts):
        out_best(k).wait_recv()
    highest = best[...]
    for k in range(1, experts):
        highest = jnp.maximum(highest, bests[k])
    top[...] = highest
    all_bests[0] = highest
    for k in range(1, dps):
        spread_best(k).start()
    add_far(groups - 2)
    add_far(groups - 1)
    own_back.wait()
    for k in range(1, dps):
        spread_best(k).wait()
    for k in range(1, experts):
        e = ahead(k)
        remote(final.at[k], back.at[e], s6.at[k], r6.at[k], a, e).wait_recv()
        home(k).wait_send()
        out(k).wait_send()
        out_best(k).wait_send()
    for k in range(experts):
        for q in range(1, nx):
            fan(q, k).wait_send()
            across(q, k).wait_send()
        for q in range(nx):
            share(q, k).wait_send()
            beside(q, k).wait_send()


def layer(packed, best, w_in, w_out, dps):
    experts, capacity, width = packed.shape
    nx = dps // 2
    ff = w_in.shape[1]
    tall = 2 * dps * capacity
    dtype = packed.dtype
    sem = pltpu.SemaphoreType.DMA
    anywhere = pl.BlockSpec(memory_space=pl.ANY)
    inside = pl.BlockSpec(memory_space=pltpu.VMEM)
    return pl.pallas_call(
        functools.partial(layer_kernel, dps, experts),
        out_shape=(
            jax.ShapeDtypeStruct((experts, capacity, width), dtype),
            jax.ShapeDtypeStruct((experts, dps, capacity, width), dtype),
            jax.ShapeDtypeStruct((experts,) + best.shape, best.dtype),
            jax.ShapeDtypeStruct((dps,) + best.shape, best.dtype),
        ),
        in_specs=[anywhere, inside, anywhere, anywhere],
        out_specs=(anywhere, anywhere, inside, inside),
        scratch_shapes=[
            pltpu.VMEM((width, ff), dtype),
            pltpu.VMEM((ff, width), dtype),
            pltpu.VMEM((2, dps, capacity, width), dtype),
            pltpu.VMEM((tall, width), dtype),
            pltpu.VMEM((tall, ff), dtype),
            pltpu.VMEM((experts, dps, capacity, width), dtype),
            pltpu.VMEM((nx, experts, capacity, width), dtype),
            pltpu.VMEM((nx - 1, experts, capacity, width), dtype),
            pltpu.VMEM((experts, capacity, width), dtype),
            pltpu.VMEM(best.shape, best.dtype),
            sem((2,)),
            sem((3,)),
            sem((experts,)),
            sem((experts,)),
            sem((nx - 1, experts)),
            sem((nx - 1, experts)),
            sem((nx, experts)),
            sem((nx, experts)),
            sem((nx, experts)),
            sem((nx, experts)),
            sem((nx - 1, experts)),
            sem((nx - 1, experts)),
            sem((experts,)),
            sem((experts,)),
            sem((experts,)),
            sem((experts,)),
            sem((dps,)),
            sem((dps,)),
        ],
        compiler_params=pltpu.CompilerParams(
            collective_id=0, has_side_effects=True, vmem_limit_bytes=63 * 1024 * 1024
        ),
        name="layer",
    )(packed, best, w_in, w_out)


def shards(tokens, router, price, w_in, w_out, assign):
    experts = router.shape[1]
    width = tokens.shape[1]
    local_tokens = tokens.shape[0]
    capacity = -(-3 * local_tokens // (2 * experts * 8)) * 8
    dp_count = lax.axis_size("dp")
    first = w_in[0]
    second = w_out[0]
    affinity = jnp.dot(tokens, router, preferred_element_type=jnp.float32)
    onehot = assign[:, None] == jnp.arange(experts, dtype=jnp.int32)[None, :]
    own = jnp.sum(jnp.where(onehot, affinity, 0.0), axis=1)
    rival = jnp.max(jnp.where(onehot, -1e30, affinity - price[None, :]), axis=1)
    bid = own - rival + BID_STEP
    local_best = jnp.max(jnp.where(onehot, bid[:, None], -1e30), axis=0)
    lower = (jnp.arange(local_tokens)[:, None] >= jnp.arange(local_tokens)[None, :]).astype(jnp.bfloat16)
    running = jnp.dot(lower, onehot.astype(jnp.bfloat16), preferred_element_type=jnp.float32)
    slots = jnp.sum(jnp.where(onehot, running, 0.0), axis=1).astype(jnp.int32) - 1
    place = assign * capacity + slots
    pack = (place[None, :] == jnp.arange(experts * capacity, dtype=jnp.int32)[:, None]).astype(jnp.bfloat16)
    packed = jnp.dot(pack, tokens, preferred_element_type=jnp.float32).astype(jnp.bfloat16)
    best = jnp.full((8, 128), -1e30, jnp.float32).at[0, :experts].set(local_best)
    returned, _, _, all_bests = layer(
        packed.reshape(experts, capacity, width), best, first, second, dp_count
    )
    new_price = jnp.max(all_bests, axis=0)[0, :experts]
    returned = returned.reshape(experts * capacity, width)
    picked = lax.dot_general(pack, returned, (((0,), (0,)), ((), ())), preferred_element_type=jnp.float32)
    gate = jax.nn.sigmoid(own)
    mixed = (gate[:, None] * picked).astype(jnp.bfloat16)
    return (mixed, new_price)


def solution(mesh):
    return jax.shard_map(
        shards,
        mesh=mesh,
        in_specs=(
            P(("dp", "expert"), None),
            P(),
            P(),
            P("expert", None, "dp"),
            P("expert", "dp", None),
            P(("dp", "expert")),
        ),
        out_specs=(P(("dp", "expert"), None), P()),
        check_vma=False,
    )
```

time: 269 us -> 139 us (0.52)
  Pallas kernels: 0 us -> 127 us
  waiting for transfers between devices: 104 us -> 0 us
  blocking collectives: 101 us -> 0 us
  matrix products: 43.6 us -> 8.32 us
  between operations: 14.1 us -> 0.67 us
  starting transfers between devices: 5.59 us -> 0 us
    pallas_call x0 -> x1, Pallas kernels: none -> 127 us  [layer(): pl.pallas_call(functools.partial(layer_kernel, dps, experts), out_shape=(...]
    reduce_scatter x1 -> x0, waiting for transfers between devices: 58.5 us -> none  [shards(): summed = lax.psum_scatter(partial, 'dp', scatter_dimension=0, tiled=True)]
    pmax x1 -> x0, blocking collectives: 56.3 us -> none  [shards(): new_price = lax.pmax(local_best, ('dp', 'expert'))]
    all_gather x1 -> x0, waiting for transfers between devices: 45.5 us -> none  [shards(): lax.all_gather(mine.reshape(experts * capacity, width), 'dp', axis=0, til...]
    all_to_all x1 -> x0, blocking collectives: 44.2 us -> none  [shards(): lax.all_to_all(packed.reshape(experts, capacity, width), 'expert', split_...]
    dot_general x1 -> x0, matrix products: 40.2 us -> none  [shards(): jnp.dot(hidden, second, preferred_element_type=jnp.float32)]
    all_to_all x1 -> x0, starting transfers between devices: 5.51 us -> none  [shards(): lax.all_to_all(summed.reshape(experts, capacity, width), 'expert', split_...]
  transfers between devices with their start and end apart: 3 -> 0, of which waited for: 2 -> 0; matrix products, arithmetic and copies ran while one was open for 0% -> 0% of each run, Pallas kernels for 0% -> 0%
where the time goes in v3:
time: 139 us
  Pallas kernels  127 us (91%)
  matrix products  8.32 us (6%)
  other arithmetic  1.47 us (1%)
    pallas_call x1, Pallas kernels, layer(): pl.pallas_call(functools.partial(layer_kernel, dps, experts), out_shape=(...  127 us
    dot_general x1, matrix products, shards(): jnp.dot(pack, tokens, preferred_element_type=jnp.float32)  2.93 us
    dot_general x1, matrix products, shards(): lax.dot_general(pack, returned, (((0,), (0,)), ((), ())), preferred_eleme...  2.88 us

profile of v3, /device:TPU:0, one launch (start us, length us, event | category | flops | bytes accessed | tf_op | source)
XLA Modules:
  0.0 138.5 jit_solution(6727864015239253913)
XLA Ops:
  0.6 0.0 copy-start
  0.6 0.9 fusion.1
  1.5 0.7 add_add_fusion
  2.2 0.0 copy-done
  2.2 1.6 %select_reduce_fusion.1 = (f32[128]{0:T(128)S(1)}, f32[128]{0:T(128)S(1)}) fusion(f32[8]{0:T(128)} %param.10, s32[128]{0:T(128)} %param.13, bf16[128,4096]{1,0:T(8,128)(2,1)} %param.8, bf16[4096,8]{0,1:T(8,128)(2,1)S(1)} %copy-done), kind=kOutput, calls=%fused_computation.10 | convolution fusion | flops 8394496 | bytes 1115680 | tf_op jit(solution)/shard_map/dot_general | solution.py:301
  3.9 0.8 select_reduce_fusion
  4.6 0.6 scatter.4.best
  5.2 2.9 %convolution_convert_fusion = bf16[192,4096]{1,0:T(8,128)(2,1)} fusion(bf16[128,4096]{1,0:T(8,128)(2,1)} %param.8, s32[128]{0:T(128)S(1)} %add_add_fusion), kind=kOutput, calls=%fused_computation | convolution fusion | flops 202137600 | bytes 2621952 | tf_op jit(solution)/shard_map/dot_general | solution.py:312
  8.2 126.9 %layer.1 = (bf16[8,24,4096]{2,1,0:T(8,128)(2,1)}, bf16[8,4,24,4096]{3,2,1,0:T(8,128)(2,1)}, f32[8,8,128]{2,1,0:T(8,128)}, f32[4,8,128]{2,1,0:T(8,128)}) custom-call(bf16[8,24,4096]{2,1,0:T(8,128)(2,1)} %bitcast.13, f32[8,128]{1,0:T(8,128)} %scatter.4.best, bf16[4096,2048]{1,0:T(8,128)(2,1)} %bitcast.11, bf16[2048,4096]{1,0:T(8,128)(2,1)} %bitcast.12), custom_call_target="tpu_custom_call" | custom-call | tf_op jit(solution)/shard_map/layer/pallas_call | solution.py:246
  135.1 0.0 copy-start.1
  135.1 2.9 %fusion = bf16[128,4096]{1,0:T(8,128)(2,1)} fusion(bf16[192,4096]{1,0:T(8,128)(2,1)} %bitcast.14, f32[128]{0:T(128)S(1)} %get-tuple-element.20, s32[128]{0:T(128)S(1)} %add_add_fusion), kind=kOutput, calls=%fused_computation.2 | convolution fusion | flops 202399744 | bytes 2622464 | tf_op jit(solution)/shard_map/dot_general | solution.py:319
  138.0 0.0 copy-done.1
  138.0 0.5 slice_bitcast_fusion
  (2 shorter events, 0.0 us)
Async XLA Ops:
  0.6 1.6 %copy-start = (bf16[4096,8]{0,1:T(8,128)(2,1)S(1)}, bf16[4096,8]{0,1:T(8,128)(2,1)}, u32[]{:S(2)}) copy-start(bf16[4096,8]{0,1:T(8,128)(2,1)} %param.9) | copy-start | bytes 196612
  135.1 2.9 %copy-start.1 = (f32[4,8,128]{2,1,0:T(8,128)S(1)}, f32[4,8,128]{2,1,0:T(8,128)}, u32[]{:S(2)}) copy-start(f32[4,8,128]{2,1,0:T(8,128)} %get-tuple-element.17) | copy-start | bytes 49156

commit v4 on v3

--- a/solution.py
+++ b/solution.py
@@ -39,17 +39,23 @@
     capacity, width = packed.shape[1:]
     ff = win.shape[1]
     cut = 512
+    wide = 1024
     tall = 2 * dps * capacity
     load_in = pltpu.make_async_copy(w_in, win, load_sem.at[0])
     load_out = pltpu.make_async_copy(w_out, wout, load_sem.at[1])
     load_in.start()
     greet(dps, experts, a, b)
 
-    def ahead(k):
-        return 2 * lax.rem(z + k // 2, groups) + lax.rem(y + k % 2, 2)
+    order = list(range(groups))
 
     def behind(k):
-        return 2 * lax.rem(z + groups - k // 2, groups) + lax.rem(y + k % 2, 2)
+        to = z
+        for bit in range(groups.bit_length()):
+            if order[k // 2] >> bit & 1:
+                to = to + (1 - 2 * lax.rem(z // 2**bit, 2)) * 2**bit
+        return 2 * to + lax.rem(y + k % 2, 2)
+
+    ahead = behind
 
     def xrow(q):
         return 2 * lax.rem(x + q, nx) + c
@@ -127,24 +133,32 @@
             return carry
 
         def first(t, carry):
-            cols = pl.ds(pl.multiple_of(t * cut, cut), cut)
+            cols = pl.ds(pl.multiple_of(t * wide, wide), wide)
             raw = jnp.dot(flat[...], win[:, cols], preferred_element_type=jnp.float32)
             hidden[:, cols] = jax.nn.gelu(raw, approximate=True).astype(jnp.bfloat16)
             return carry
 
         def second(t, carry):
-            cols = pl.ds(pl.multiple_of(t * cut, cut), cut)
+            cols = pl.ds(pl.multiple_of(t * wide, wide), wide)
             res = jnp.dot(hidden[...], wout[:, cols], preferred_element_type=jnp.float32)
-            part[2 * g : 2 * g + 2, :, :, cols] = res.reshape(2, dps, capacity, cut).astype(jnp.bfloat16)
+            part[2 * g : 2 * g + 2, :, :, cols] = res.reshape(2, dps, capacity, wide).astype(jnp.bfloat16)
             return carry
 
         lax.fori_loop(0, width // cut, flatten, 0)
         if g == 0:
             load_in.wait()
-        lax.fori_loop(0, ff // cut, first, 0)
+        lax.fori_loop(0, ff // wide, first, 0)
+        if g + 2 < groups:
+            arrive(g + 2)
+        if g + 1 < groups:
+            forward(g + 1)
+        if g >= 1:
+            add_pair(g - 1)
+        if g >= 2:
+            add_far(g - 2)
         if g == 0:
             load_out.wait()
-        lax.fori_loop(0, width // cut, second, 0)
+        lax.fori_loop(0, width // wide, second, 0)
         for q in list(range(1, nx)) + [0]:
             for k in (2 * g, 2 * g + 1):
                 beside(q, k).start()
@@ -196,14 +210,6 @@
     forward(0)
     for g in range(groups):
         compute(g)
-        if g + 2 < groups:
-            arrive(g + 2)
-        if g + 1 < groups:
-            forward(g + 1)
-        if g >= 1:
-            add_pair(g - 1)
-        if g >= 2:
-            add_far(g - 2)
     add_pair(groups - 1)
     for k in range(1, experts):
         out_best(k).wait_recv()

time: 139 us -> 125 us (0.90)
  the two profiles are of different devices: /device:TPU:0 before, /device:TPU:8 now
where the time goes in v4:
time: 125 us
  Pallas kernels  113 us (90%)
  matrix products  8.32 us (7%)
  other arithmetic  1.47 us (1%)
    pallas_call x1, Pallas kernels, layer(): pl.pallas_call(functools.partial(layer_kernel, dps, experts), out_shape=(...  113 us
    dot_general x1, matrix products, shards(): jnp.dot(pack, tokens, preferred_element_type=jnp.float32)  2.93 us
    dot_general x1, matrix products, shards(): lax.dot_general(pack, returned, (((0,), (0,)), ((), ())), preferred_eleme...  2.87 us

profile of v4, /device:TPU:8, one launch (start us, length us, event | category | flops | bytes accessed | tf_op | source)
XLA Modules:
  0.0 124.5 jit_solution(14502154546227589382)
XLA Ops:
  0.6 0.0 copy-start
  0.6 0.9 fusion.1
  1.5 0.7 add_add_fusion
  2.2 0.0 copy-done
  2.2 1.6 %select_reduce_fusion.1 = (f32[128]{0:T(128)S(1)}, f32[128]{0:T(128)S(1)}) fusion(f32[8]{0:T(128)} %param.10, s32[128]{0:T(128)} %param.13, bf16[128,4096]{1,0:T(8,128)(2,1)} %param.8, bf16[4096,8]{0,1:T(8,128)(2,1)S(1)} %copy-done), kind=kOutput, calls=%fused_computation.10 | convolution fusion | flops 8394496 | bytes 1115680 | tf_op jit(solution)/shard_map/dot_general | solution.py:307
  3.9 0.8 select_reduce_fusion
  4.6 0.6 scatter.4.best
  5.2 2.9 %convolution_convert_fusion = bf16[192,4096]{1,0:T(8,128)(2,1)} fusion(bf16[128,4096]{1,0:T(8,128)(2,1)} %param.8, s32[128]{0:T(128)S(1)} %add_add_fusion), kind=kOutput, calls=%fused_computation | convolution fusion | flops 202137600 | bytes 2621952 | tf_op jit(solution)/shard_map/dot_general | solution.py:318
  8.2 112.9 %layer.1 = (bf16[8,24,4096]{2,1,0:T(8,128)(2,1)}, bf16[8,4,24,4096]{3,2,1,0:T(8,128)(2,1)}, f32[8,8,128]{2,1,0:T(8,128)}, f32[4,8,128]{2,1,0:T(8,128)}) custom-call(bf16[8,24,4096]{2,1,0:T(8,128)(2,1)} %bitcast.13, f32[8,128]{1,0:T(8,128)} %scatter.4.best, bf16[4096,2048]{1,0:T(8,128)(2,1)} %bitcast.11, bf16[2048,4096]{1,0:T(8,128)(2,1)} %bitcast.12), custom_call_target="tpu_custom_call" | custom-call | tf_op jit(solution)/shard_map/layer/pallas_call | solution.py:252
  121.1 0.0 copy-start.1
  121.1 2.9 %fusion = bf16[128,4096]{1,0:T(8,128)(2,1)} fusion(bf16[192,4096]{1,0:T(8,128)(2,1)} %bitcast.14, f32[128]{0:T(128)S(1)} %get-tuple-element.20, s32[128]{0:T(128)S(1)} %add_add_fusion), kind=kOutput, calls=%fused_computation.2 | convolution fusion | flops 202399744 | bytes 2622464 | tf_op jit(solution)/shard_map/dot_general | solution.py:325
  124.0 0.0 copy-done.1
  124.0 0.5 slice_bitcast_fusion
  (2 shorter events, 0.0 us)
Async XLA Ops:
  0.6 1.6 %copy-start = (bf16[4096,8]{0,1:T(8,128)(2,1)S(1)}, bf16[4096,8]{0,1:T(8,128)(2,1)}, u32[]{:S(2)}) copy-start(bf16[4096,8]{0,1:T(8,128)(2,1)} %param.9) | copy-start | bytes 196612
  121.1 2.9 %copy-start.1 = (f32[4,8,128]{2,1,0:T(8,128)S(1)}, f32[4,8,128]{2,1,0:T(8,128)}, u32[]{:S(2)}) copy-start(f32[4,8,128]{2,1,0:T(8,128)} %get-tuple-element.17) | copy-start | bytes 49156
